TPU v7x, 256 devices: a whole 4x4x8 slice. The times are simulated.
256 devices in a mesh: dp: 32 (over x, z), section: 8 (over y, core).
Axes of the slice: x: 4, y: 4, z: 8, core: 2. Of those that a mesh axis runs over, the one named last changes fastest.
Arguments:
- tap_maps: bfloat16 [4, 2, 4096, 3200], P(None, None, ('dp', 'section')), may hold values from -6 to 6
- lateral_weight: bfloat16 [8, 3200, 768], P('section', 'dp'), may hold values from -0.109375 to 0.109375
- conv_weight: bfloat16 [8, 6912, 768], P('section'), may hold values from -0.078125 to 0.078125
- classifier: bfloat16 [768, 150], replicated, may hold values from -0.875 to 0.875
- tile_counts: int32 [32, 2], P('dp'), may hold values from 1 to 2, as said below
- labels: int32 [2, 4096], P(None, 'dp'), may hold values from 0 to 149
Outputs:
- conv_grad: float32 [8, 6912, 768], P('section', 'dp')
- lateral_grad: float32 [8, 3200, 768], P('section', 'dp')
Inputs may be any that keep to these rules, and one draw needn't show every extreme that they name: `tile_counts`: some entry equals 2.
All inputs are finite; a program needn't handle non-finite values.
Results may differ from a plain program's by a relative error of at most 0.035.
Values may be sent and summed in bfloat16 or wider, within the bound.
A program may use at most 128 MiB of HBM per device.

v0:
```python
import jax
import jax.numpy as jnp
from jax import lax
from jax.sharding import PartitionSpec as P

TILE_CAP = 2
BAND_ROWS = 1
BAND_COLS = 64


def padded_2(shard, sides, width):
    for axis, dim in sides:
        size, length = (lax.axis_size(axis), shard.shape[dim])
        up = [(i, (i + 1) % size) for i in range(size - 1)]
        down = [(j, i) for i, j in up]
        last = lax.slice_in_dim(shard, length - width, length, axis=dim)
        initial = lax.slice_in_dim(shard, 0, width, axis=dim)
        before = lax.ppermute(last, axis, up)
        after = lax.ppermute(initial, axis, down)
        shard = jnp.concatenate([before, shard, after], axis=dim)
    return shard


def shifted(block, axis, distance):
    devices = range(lax.axis_size(axis))
    route = [(i - distance, i) for i in devices if i - distance in devices]
    return lax.ppermute(block, axis, route)


def neighbour_shifts():
    return [(row_shift, col_shift) for row_shift in (-1, 0, 1) for col_shift in (-1, 0, 1)]


def widen(summed):
    grid = summed.reshape(TILE_CAP, BAND_ROWS, BAND_COLS, summed.shape[-1])
    return padded_2(grid, (("dp", 1),), 1)


def gather_columns(widened):
    chans = widened.shape[-1]
    padded = jnp.pad(widened, ((0, 0), (0, 0), (1, 1), (0, 0)))
    pieces = [
        padded[:, 1 + rs : 1 + rs + BAND_ROWS, 1 + cs : 1 + cs + BAND_COLS, :]
        for rs, cs in neighbour_shifts()
    ]
    return jnp.concatenate(pieces, axis=-1).reshape(-1, 9 * chans)


def spread_columns(grad_cols):
    chans = grad_cols.shape[-1] // 9
    grid = grad_cols.reshape(TILE_CAP, BAND_ROWS, BAND_COLS, 9, chans)
    total = jnp.zeros((TILE_CAP, BAND_ROWS + 2, BAND_COLS + 2, chans), jnp.float32)
    for offset, (rs, cs) in enumerate(neighbour_shifts()):
        total = total + jnp.pad(
            grid[:, :, :, offset, :], ((0, 0), (1 + rs, 1 - rs), (1 + cs, 1 - cs), (0, 0))
        )
    inner = total[:, 1:-1, 1:-1, :]
    rims = jnp.stack([total[:, 0, 1:-1, :], total[:, BAND_ROWS + 1, 1:-1, :]], axis=1)
    return (inner, rims)


def on_device(tap_maps, lateral_weight, conv_weight, classifier, tile_counts, labels):
    sections = lax.axis_size("section")
    groups = lax.axis_size("dp")
    place = lax.axis_index("section")
    levels = tap_maps.shape[0]
    micros = tap_maps.shape[1]
    width = tap_maps.shape[3]
    pixels = labels.shape[1]
    chans = conv_weight.shape[2]
    classes = classifier.shape[1]
    gathered = lax.all_gather(tap_maps, "section", axis=2, tiled=True)
    routed = lax.dynamic_index_in_dim(gathered, place * levels // sections, 0, keepdims=False)
    tap_rows = routed.reshape(micros * pixels, width)
    left = tap_rows
    lateral = jnp.dot(
        left,
        lax.all_gather(lateral_weight[0], "dp", axis=0, tiled=True),
        preferred_element_type=jnp.float32,
    )
    lateral = lateral.reshape(micros, pixels, chans)
    weights = conv_weight[0]
    ticks = sections + micros - 1

    def forward(step_count, carry):
        outgoing, widened_store, preact_store = carry
        incoming = shifted(outgoing, "section", 1)
        micro = step_count - place
        active = jnp.logical_and(micro >= 0, micro < micros)
        which = jnp.clip(micro, 0, micros - 1)
        summed = (
            incoming.astype(jnp.float32)
            + lax.dynamic_index_in_dim(lateral, which, 0, keepdims=False)
        ).astype(jnp.bfloat16)
        widened = widen(summed)

        def forward_advance(operands):
            extended, widened_old, preact_old = operands
            preact = jnp.dot(gather_columns(extended), weights, preferred_element_type=jnp.float32)
            activated = jax.nn.silu(preact).astype(jnp.bfloat16)
            return (
                activated,
                lax.dynamic_update_index_in_dim(widened_old, extended, which, 0),
                lax.dynamic_update_index_in_dim(preact_old, preact, which, 0),
            )

        def forward_skipped(operands):
            return (jnp.zeros((pixels, chans), jnp.bfloat16), operands[1], operands[2])

        return lax.cond(
            active, forward_advance, forward_skipped, (widened, widened_store, preact_store)
        )

    start_state = (
        jnp.zeros((pixels, chans), jnp.bfloat16),
        jnp.zeros((micros, TILE_CAP, BAND_ROWS + 2, BAND_COLS, chans), jnp.bfloat16),
        jnp.zeros((micros, pixels, chans), jnp.float32),
    )
    _, widened_store, preact_store = lax.fori_loop(0, ticks, forward, start_state)
    band = BAND_ROWS * BAND_COLS
    slot_ids = jnp.arange(pixels) // band
    per_count = tile_counts[0][:, None]
    valid = (slot_ids[None, :] < per_count).astype(jnp.float32)
    pixel_weight = valid / (per_count.astype(jnp.float32) * band * groups * micros)
    is_last = place == sections - 1
    class_ids = jnp.arange(classes)

    def backward(step_count, carry):
        outgoing, grad_pre_store, grad_in_store = carry
        incoming = shifted(outgoing, "section", -1)
        micro = step_count - (sections - 1 - place)
        active = jnp.logical_and(micro >= 0, micro < micros)
        which = jnp.clip(micro, 0, micros - 1)

        def backward_advance(operands):
            arrived, grad_pre_old = operands
            preact = lax.dynamic_index_in_dim(preact_store, which, 0, keepdims=False)
            activated = jax.nn.silu(preact).astype(jnp.bfloat16)
            logits = jnp.dot(activated, classifier, preferred_element_type=jnp.float32)
            expo = jnp.exp(logits)
            probs = expo / jnp.sum(expo, axis=-1, keepdims=True)
            label_row = lax.dynamic_index_in_dim(labels, which, 0, keepdims=False)
            onehot = (label_row[:, None] == class_ids[None, :]).astype(jnp.float32)
            weight_row = lax.dynamic_index_in_dim(pixel_weight, which, 0, keepdims=False)
            grad_logits = ((probs - onehot) * weight_row[:, None]).astype(jnp.bfloat16)
            from_loss = lax.dot_general(
                grad_logits,
                classifier,
                (((1,), (1,)), ((), ())),
                preferred_element_type=jnp.float32,
            )
            grad_out = jnp.where(is_last, from_loss, arrived.astype(jnp.float32))
            sigma = jax.nn.sigmoid(preact)
            grad_pre = (grad_out * sigma * (1.0 + preact * (1.0 - sigma))).astype(jnp.bfloat16)
            grad_cols = lax.dot_general(
                grad_pre, weights, (((1,), (1,)), ((), ())), preferred_element_type=jnp.float32
            )
            inner, rims = spread_columns(grad_cols)
            return (inner, rims, lax.dynamic_update_index_in_dim(grad_pre_old, grad_pre, which, 0))

        def backward_skipped(operands):
            return (
                jnp.zeros((TILE_CAP, BAND_ROWS, BAND_COLS, chans), jnp.float32),
                jnp.zeros((TILE_CAP, 2, BAND_COLS, chans), jnp.float32),
                operands[1],
            )

        inner, rims, grad_pre_store = lax.cond(
            active, backward_advance, backward_skipped, (incoming, grad_pre_store)
        )
        received = padded_2(rims.astype(jnp.bfloat16), (("dp", 1),), 1).astype(rims.dtype)
        inner = inner.at[:, 0].add(received[:, 0])
        inner = inner.at[:, BAND_ROWS - 1].add(received[:, 3])
        grad_in = inner.reshape(pixels, chans).astype(jnp.bfloat16)
        updated = lax.dynamic_update_index_in_dim(grad_in_store, grad_in, which, 0)
        grad_in_store = jnp.where(active, updated, grad_in_store)
        return (grad_in, grad_pre_store, grad_in_store)

    back_state = (
        jnp.zeros((pixels, chans), jnp.bfloat16),
        jnp.zeros((micros, pixels, chans), jnp.bfloat16),
        jnp.zeros((micros, pixels, chans), jnp.bfloat16),
    )
    _, grad_pre_store, grad_in_store = lax.fori_loop(0, ticks, backward, back_state)
    grad_pre_rows = grad_pre_store.reshape(micros * pixels, chans)
    grad_in_rows = grad_in_store.reshape(micros * pixels, chans)
    column_rows = gather_columns(
        widened_store.reshape(micros * TILE_CAP, BAND_ROWS + 2, BAND_COLS, chans)
    )
    left = tap_rows
    lateral_grad = lax.psum_scatter(
        lax.dot_general(
            left, grad_in_rows, (((0,), (0,)), ((), ())), preferred_element_type=jnp.float32
        ).astype(jnp.bfloat16),
        "dp",
        scatter_dimension=0,
        tiled=True,
    ).astype(jnp.float32)
    left = column_rows
    conv_grad = lax.psum_scatter(
        lax.dot_general(
            left, grad_pre_rows, (((0,), (0,)), ((), ())), preferred_element_type=jnp.float32
        ).astype(jnp.bfloat16),
        "dp",
        scatter_dimension=0,
        tiled=True,
    ).astype(jnp.float32)
    return (conv_grad[None], lateral_grad[None])


def solution(mesh):
    placed = (
        P(None, None, ("dp", "section"), None),
        P("section", "dp", None),
        P("section", None, None),
        P(),
        P("dp", None),
        P(None, "dp"),
    )
    return jax.shard_map(
        on_device,
        mesh=mesh,
        in_specs=placed,
        out_specs=(P("section", "dp", None), P("section", "dp", None)),
        check_vma=False,
    )
```

profile of v0, /device:TPU:8, one launch (start us, length us, event | category | flops | bytes accessed | tf_op | source)
XLA Modules:
  0.0 1171.2 jit_solution(1554315526162453511)
XLA Ops:
  10.9 45.6 %all-gather.4.cloned.1.call-done = bf16[4,2,128,3200]{3,2,1,0:T(8,128)(2,1)} async-done(((bf16[4,2,16,3200]{3,2,1,0:T(8,128)(2,1)}), bf16[4,2,128,3200]{3,2,1,0:T(8,128)(2,1)}) %all-gather.4.cloned.1.call-update) | async-done | bytes 6553616 | tf_op jit(solution)/shard_map/all_gather | solution.py:72
  58.0 108.3 %all-gather.6.cloned.1.call-done = bf16[1,3200,768]{2,0,1:T(2,128)(2,1)} async-done(((bf16[1,100,768]{2,0,1:T(2,128)(2,1)}), bf16[1,3200,768]{2,0,1:T(2,128)(2,1)}) %all-gather.6.cloned.1.call-update) | async-done | bytes 4915216 | tf_op jit(solution)/shard_map/all_gather | solution.py:78
  173.3 192.2 %while.43 = (s32[]{:T(128)}, bf16[128,768]{1,0:T(8,128)(2,1)}, bf16[2,2,3,64,768]{4,3,2,1,0:T(8,128)(2,1)S(1)}, f32[2,128,768]{2,1,0:T(8,128)}, s32[]{:T(128)}, ...) while((s32[]{:T(128)}, bf16[128,768]{1,0:T(8,128)(2,1)}, ...), condition=%wide.region_3.4_spmd, body=%wide.region_0.3_spmd.sunk | while | flops 1360330752 | bytes 25166232 | solution.py:119
  212.7 9.7 collective-permute-done
  234.0 7.6 conditional.5
  234.5 6.3 multiply_convert_fusion
  260.3 7.6 conditional.5
  260.7 6.3 multiply_convert_fusion
  325.8 6.5 collective-permute-start
  345.9 5.9 collective-permute-start
  369.7 504.1 %while.44 = (s32[]{:T(128)}, bf16[128,768]{1,0:T(8,128)(2,1)S(1)}, bf16[2,128,768]{2,1,0:T(8,128)(2,1)}, bf16[2,128,768]{2,1,0:T(8,128)(2,1)}, s32[]{:T(128)}, /...) while((s32[]{:T(128)}, bf16[128,768]{1,0:T(8,128)(2,1)S(1)}, ...), condition=%wide.region_8.9_spmd.clone, body=%wide.region_4.8_spmd.clone.sunk | while | flops 1424437120 | bytes 46599908 | solution.py:184
  398.9 5.9 collective-permute-done.3
  426.6 6.0 collective-permute-done.3
  454.4 6.9 collective-permute-done.3
  493.6 6.0 collective-permute-start.5
  511.5 161.1 %collective-permute-done.3 = bf16[128,768]{1,0:T(8,128)(2,1)S(1)} collective-permute-done((bf16[128,768]{1,0:T(8,128)(2,1)S(1)}, bf16[128,768]{1,0:T(8,128)(2,1)S(1)}, u32[]{:S(2)}, u32[]{:S(2)}) %collective-permute-start.3) | collective-permute-done | bytes 196640 | tf_op jit(solution)/shard_map/while/body/eval_jaxpr/ppermute | solution.py:27
  672.6 34.2 %conditional.6 = (f32[2,1,64,768]{3,1,2,0:T(1,128)}, bf16[2,2,64,768]{3,1,2,0:T(2,128)(2,1)}, bf16[2,128,768]{2,1,0:T(8,128)(2,1)}) conditional(s32[]{:T(128)} %convert_element_type.205, bf16[2,128,768]{2,1,0:T(8,128)(2,1)} %get-tuple-element.928, (pred[]{:T(512)}, s32[]{:T(128)}, f32[2,128,768]{2,1,0:T(8,128)}, bf16[768,150]{1,0:T(8,128)(2,1)}, ...), branch_computations={%region_5.5_spmd, %region_6.7_spmd} | conditional | flops 1422863744 | bytes 37946536 | solution.py:168
  677.0 7.5 fusion.47
  687.8 12.8 %slice_bitcast_fusion.8 = (f32[2,1,64,768]{3,1,2,0:T(1,128)S(1)}, f32[2,1,64,768]{3,1,2,0:T(1,128)S(1)}, f32[2,1,64,768]{3,1,2,0:T(1,128)S(1)}, f32[2,1,64,768]{...) fusion(f32[2,1,64,9,768]{4,3,2,0,1:T(8,128)} %reshape.209), kind=kLoop, calls=%fused_computation.38 | loop fusion | bytes 7077888 | tf_op jit(solution)/shard_map/while/body/eval_jaxpr/cond/branch_1_fun/squeeze | solution.py:55
  710.0 6.2 collective-permute-start.5
  733.4 34.2 %conditional.6 = (f32[2,1,64,768]{3,1,2,0:T(1,128)}, bf16[2,2,64,768]{3,1,2,0:T(2,128)(2,1)}, bf16[2,128,768]{2,1,0:T(8,128)(2,1)}) conditional(s32[]{:T(128)} %convert_element_type.205, bf16[2,128,768]{2,1,0:T(8,128)(2,1)} %get-tuple-element.928, (pred[]{:T(512)}, s32[]{:T(128)}, f32[2,128,768]{2,1,0:T(8,128)}, bf16[768,150]{1,0:T(8,128)(2,1)}, ...), branch_computations={%region_5.5_spmd, %region_6.7_spmd} | conditional | flops 1422863744 | bytes 37946536 | solution.py:168
  737.8 7.5 fusion.47
  748.5 12.8 %slice_bitcast_fusion.8 = (f32[2,1,64,768]{3,1,2,0:T(1,128)S(1)}, f32[2,1,64,768]{3,1,2,0:T(1,128)S(1)}, f32[2,1,64,768]{3,1,2,0:T(1,128)S(1)}, f32[2,1,64,768]{...) fusion(f32[2,1,64,9,768]{4,3,2,0,1:T(8,128)} %reshape.209), kind=kLoop, calls=%fused_computation.38 | loop fusion | bytes 7077888 | tf_op jit(solution)/shard_map/while/body/eval_jaxpr/cond/branch_1_fun/squeeze | solution.py:55
  770.7 5.9 collective-permute-start.5
  796.9 6.3 collective-permute-start.5
  803.1 5.7 collective-permute-done.4
  814.8 34.6 %collective-permute-start.3 = (bf16[128,768]{1,0:T(8,128)(2,1)S(1)}, bf16[128,768]{1,0:T(8,128)(2,1)S(1)}, u32[]{:S(2)}, u32[]{:S(2)}) collective-permute-start(bf16[128,768]{1,0:T(8,128)(2,1)S(1)} %get-tuple-element.927), channel_id=1, source_target_pairs={{1,0},{2,1},{3,2},{4,3},{5,4},{6,5},{7,6},{9,8},{10,9},{11,10},{12... | collective-permute-start | bytes 589832 | tf_op jit(solution)/shard_map/while/body/eval_jaxpr/ppermute | solution.py:27
  857.6 5.9 collective-permute-start.5
  863.5 5.5 collective-permute-done.4
  873.8 9.1 convolution_convert_fusion
  888.2 111.0 %fusion.4 = bf16[104,768]{1,0:T(8,128)(2,1)S(1)} fusion(bf16[3200,768]{1,0:T(8,128)(2,1)} %convolution_convert_fusion.1), kind=kCustom, calls=%all-reduce-scatter | all-reduce-scatter fusion | flops 2555905 | bytes 5075968
  1007.1 155.7 %reduce-scatter.4.cloned.1.call-done = bf16[216,768]{1,0:T(8,128)(2,1)} async-done(((bf16[6912,768]{1,0:T(8,128)(2,1)}), bf16[216,768]{1,0:T(8,128)(2,1)}) %reduce-scatter.4.cloned.1.call-update) | async-done | bytes 331792 | tf_op jit(solution)/shard_map/reduce_scatter | solution.py:200
  (330 shorter events, 412.5 us)
Async XLA Ops:
  7.2 49.3 %all-gather.4.cloned.1.call-start = ((), (), s32[]{:S(2)}) async-start(), calls=%async_computation.1 | async-start | bytes 7372800 | tf_op jit(solution)/shard_map/all_gather | solution.py:72
  7.9 158.4 %all-gather.6.cloned.1.call-start = ((), (), s32[]{:S(2)}) async-start(), calls=%async_computation.3 | async-start | bytes 10137600 | tf_op jit(solution)/shard_map/all_gather | solution.py:78
  9.9 1152.9 %reduce-scatter.4.cloned.1.call-start = ((), (), s32[]{:S(2)}) async-start(), calls=%async_computation.2 | async-start | bytes 10948608 | tf_op jit(solution)/shard_map/reduce_scatter | solution.py:200
  182.3 7.6 collective-permute-start.1
  198.0 7.7 collective-permute-start.2
  210.8 11.6 collective-permute-start
  297.0 8.1 collective-permute-start.1
  325.8 7.7 collective-permute-start
  357.2 7.6 collective-permute-start.1
  380.9 9.8 collective-permute-start.4
  382.2 9.9 collective-permute-start.5
  396.9 7.9 collective-permute-start.3
  408.5 9.8 collective-permute-start.4
  409.8 10.0 collective-permute-start.5
  424.6 8.0 collective-permute-start.3
  436.3 9.8 collective-permute-start.4
  437.6 10.0 collective-permute-start.5
  452.4 8.9 collective-permute-start.3
  465.1 10.7 collective-permute-start.4
  466.4 11.1 collective-permute-start.5
  492.3 11.1 collective-permute-start.4
  493.6 11.2 collective-permute-start.5
  509.5 163.1 %collective-permute-start.3 = (bf16[128,768]{1,0:T(8,128)(2,1)S(1)}, bf16[128,768]{1,0:T(8,128)(2,1)S(1)}, u32[]{:S(2)}, u32[]{:S(2)}) collective-permute-start(bf16[128,768]{1,0:T(8,128)(2,1)S(1)} %get-tuple-element.927), channel_id=1, source_target_pairs={{1,0},{2,1},{3,2},{4,3},{5,4},{6,5},{7,6},{9,8},{10,9},{11,10},{12... | collective-permute-start | bytes 589832 | tf_op jit(solution)/shard_map/while/body/eval_jaxpr/ppermute | solution.py:27
  708.7 11.9 %collective-permute-start.4 = (bf16[2,1,64,768]{3,1,2,0:T(2,128)(2,1)S(1)}, bf16[2,1,64,768]{3,1,2,0:T(2,128)(2,1)S(1)}, u32[]{:S(2)}, u32[]{:S(2)}) collective-permute-start(bf16[2,1,64,768]{3,1,2,0:T(2,128)(2,1)S(1)} %get-tuple-element.864), channel_id=1, source_target_pairs={{8,0},{16,8},{24,16},{32,24},{40,32},{48,40},{56,48},{64,56},{72,6... | collective-permute-start | bytes 589832 | tf_op jit(solution)/shard_map/while/body/eval_jaxpr/ppermute | solution.py:19
  710.0 12.4 %collective-permute-start.5 = (bf16[2,1,64,768]{3,1,2,0:T(2,128)(2,1)S(1)}, bf16[2,1,64,768]{3,1,2,0:T(2,128)(2,1)S(1)}, u32[]{:S(2)}, u32[]{:S(2)}) collective-permute-start(bf16[2,1,64,768]{3,1,2,0:T(2,128)(2,1)S(1)} %get-tuple-element.865), channel_id=1, source_target_pairs={{0,8},{8,16},{16,24},{24,32},{32,40},{40,48},{48,56},{56,64},{64,7... | collective-permute-start | bytes 589832 | tf_op jit(solution)/shard_map/while/body/eval_jaxpr/ppermute | solution.py:18
  769.4 11.0 collective-permute-start.4
  770.7 11.2 collective-permute-start.5
  795.6 13.3 %collective-permute-start.4 = (bf16[2,1,64,768]{3,1,2,0:T(2,128)(2,1)S(1)}, bf16[2,1,64,768]{3,1,2,0:T(2,128)(2,1)S(1)}, u32[]{:S(2)}, u32[]{:S(2)}) collective-permute-start(bf16[2,1,64,768]{3,1,2,0:T(2,128)(2,1)S(1)} %get-tuple-element.864), channel_id=1, source_target_pairs={{8,0},{16,8},{24,16},{32,24},{40,32},{48,40},{56,48},{64,56},{72,6... | collective-permute-start | bytes 589832 | tf_op jit(solution)/shard_map/while/body/eval_jaxpr/ppermute | solution.py:19
  796.9 13.2 %collective-permute-start.5 = (bf16[2,1,64,768]{3,1,2,0:T(2,128)(2,1)S(1)}, bf16[2,1,64,768]{3,1,2,0:T(2,128)(2,1)S(1)}, u32[]{:S(2)}, u32[]{:S(2)}) collective-permute-start(bf16[2,1,64,768]{3,1,2,0:T(2,128)(2,1)S(1)} %get-tuple-element.865), channel_id=1, source_target_pairs={{0,8},{8,16},{16,24},{24,32},{32,40},{40,48},{48,56},{56,64},{64,7... | collective-permute-start | bytes 589832 | tf_op jit(solution)/shard_map/while/body/eval_jaxpr/ppermute | solution.py:18
  814.8 37.7 %collective-permute-start.3 = (bf16[128,768]{1,0:T(8,128)(2,1)S(1)}, bf16[128,768]{1,0:T(8,128)(2,1)S(1)}, u32[]{:S(2)}, u32[]{:S(2)}) collective-permute-start(bf16[128,768]{1,0:T(8,128)(2,1)S(1)} %get-tuple-element.927), channel_id=1, source_target_pairs={{1,0},{2,1},{3,2},{4,3},{5,4},{6,5},{7,6},{9,8},{10,9},{11,10},{12... | collective-permute-start | bytes 589832 | tf_op jit(solution)/shard_map/while/body/eval_jaxpr/ppermute | solution.py:27
  856.3 12.7 %collective-permute-start.4 = (bf16[2,1,64,768]{3,1,2,0:T(2,128)(2,1)S(1)}, bf16[2,1,64,768]{3,1,2,0:T(2,128)(2,1)S(1)}, u32[]{:S(2)}, u32[]{:S(2)}) collective-permute-start(bf16[2,1,64,768]{3,1,2,0:T(2,128)(2,1)S(1)} %get-tuple-element.864), channel_id=1, source_target_pairs={{8,0},{16,8},{24,16},{32,24},{40,32},{48,40},{56,48},{64,56},{72,6... | collective-permute-start | bytes 589832 | tf_op jit(solution)/shard_map/while/body/eval_jaxpr/ppermute | solution.py:19
  857.6 11.4 collective-permute-start.5
  (52 other events, 596.3 us)
Sparse Core Ops, SparseCore 0:
  9.9 46.5 all-gather.3
  59.6 106.6 all-gather.5
  883.1 279.6 reduce-scatter.3
where the time goes:
time: 1170 us
  waiting for transfers between devices  663 us (57%)
  starting transfers between devices  185 us (16%)
  blocking collectives  111 us (9%)
  local copies, waits for them, and re-layouts  94.6 us (8%)
  matrix products  53 us (5%)
  other arithmetic  48.3 us (4%)
  between operations  14.6 us (1%)
    ppermute x18, waiting for transfers between devices, shifted(): return lax.ppermute(block, axis, route)  242 us
    reduce_scatter x1, waiting for transfers between devices, on_device(): lax.psum_scatter(lax.dot_general(left, grad_pre_rows, (((0,), (0,)), ((),...  156 us
    unnamed x1, blocking collectives  111 us
    all_gather x1, waiting for transfers between devices, on_device(): lax.all_gather(lateral_weight[0], 'dp', axis=0, tiled=True)  108 us
    ppermute x18, starting transfers between devices, padded_2(): before = lax.ppermute(last, axis, up)  82.1 us
    ppermute x18, waiting for transfers between devices, padded_2(): after = lax.ppermute(initial, axis, down)  78 us
    ppermute x18, starting transfers between devices, shifted(): return lax.ppermute(block, axis, route)  77.3 us
    all_gather x1, waiting for transfers between devices, on_device(): gathered = lax.all_gather(tap_maps, 'section', axis=2, tiled=True)  45.6 us
  transfers between devices with their start and end apart: 59, of which 57 were waited for; matrix products, arithmetic and copies ran while one was open for 10% of the time, Pallas kernels for 0%

commit v1 on v0

--- a/solution.py
+++ b/solution.py
@@ -69,7 +69,30 @@
     pixels = labels.shape[1]
     chans = conv_weight.shape[2]
     classes = classifier.shape[1]
-    gathered = lax.all_gather(tap_maps, "section", axis=2, tiled=True)
+    devices_2, index, width_2 = (
+        lax.axis_size("section"),
+        lax.axis_index("section"),
+        tap_maps.shape[2],
+    )
+    forward_2 = [(i_2, (i_2 + 1) % devices_2) for i_2 in range(devices_2)]
+    downward = [(i_2, (i_2 - 1) % devices_2) for i_2 in range(devices_2)]
+    out = jnp.zeros(
+        (*tap_maps.shape[:2], devices_2 * width_2, *tap_maps.shape[2 + 1 :]), tap_maps.dtype
+    )
+    out = lax.dynamic_update_slice_in_dim(out, tap_maps, index * width_2, axis=2)
+    from_left = from_right = tap_maps
+    middle = devices_2 // 2
+    for turn in range(1, middle + 1):
+        from_left = lax.ppermute(from_left, "section", forward_2)
+        out = lax.dynamic_update_slice_in_dim(
+            out, from_left, (index - turn) % devices_2 * width_2, axis=2
+        )
+        if turn < devices_2 - middle:
+            from_right = lax.ppermute(from_right, "section", downward)
+            out = lax.dynamic_update_slice_in_dim(
+                out, from_right, (index + turn) % devices_2 * width_2, axis=2
+            )
+    gathered = out
     routed = lax.dynamic_index_in_dim(gathered, place * levels // sections, 0, keepdims=False)
     tap_rows = routed.reshape(micros * pixels, width)
     left = tap_rows

time: 1170 us -> 1120 us (0.957)
  waiting for transfers between devices: 663 us -> 579 us
  starting transfers between devices: 185 us -> 214 us
    all_gather x1 -> x0, waiting for transfers between devices: 45.6 us -> none  [on_device(): gathered = lax.all_gather(tap_maps, 'section', axis=2, tiled=True)]
    all_gather x1, waiting for transfers between devices: 108 us -> 63 us  [on_device(): lax.all_gather(lateral_weight[0], 'dp', axis=0, tiled=True)]
    ppermute x0 -> x7, waiting for transfers between devices: none -> 36.9 us  [the longest x4 36.3 us: on_device(): from_left = lax.ppermute(from_left, 'section', forward_2)]
    ppermute x18, waiting for transfers between devices: 78 us -> 55.9 us  [padded_2(): after = lax.ppermute(initial, axis, down)]
    ppermute x18, starting transfers between devices: 82.1 us -> 103 us  [padded_2(): before = lax.ppermute(last, axis, up)]
  transfers between devices with their start and end apart: 59 -> 65, of which waited for: 57 -> 63; matrix products, arithmetic and copies ran while one was open for 10% -> 11% of each run, Pallas kernels for 0% -> 0%
where the time goes in v1:
time: 1120 us
  waiting for transfers between devices  579 us (52%)
  starting transfers between devices  214 us (19%)
  blocking collectives  114 us (10%)
  local copies, waits for them, and re-layouts  95.2 us (8%)
  matrix products  53 us (5%)
  other arithmetic  48.9 us (4%)
  between operations  15 us (1%)
    ppermute x18, waiting for transfers between devices, shifted(): return lax.ppermute(block, axis, route)  241 us
    reduce_scatter x1, waiting for transfers between devices, on_device(): lax.psum_scatter(lax.dot_general(left, grad_pre_rows, (((0,), (0,)), ((),...  155 us
    unnamed x1, blocking collectives  114 us
    ppermute x18, starting transfers between devices, padded_2(): before = lax.ppermute(last, axis, up)  103 us
    ppermute x18, starting transfers between devices, shifted(): return lax.ppermute(block, axis, route)  78.2 us
    all_gather x1, waiting for transfers between devices, on_device(): lax.all_gather(lateral_weight[0], 'dp', axis=0, tiled=True)  63 us
    ppermute x18, waiting for transfers between devices, padded_2(): after = lax.ppermute(initial, axis, down)  55.9 us
    ppermute x4, waiting for transfers between devices, on_device(): from_left = lax.ppermute(from_left, 'section', forward_2)  36.3 us
  transfers between devices with their start and end apart: 65, of which 63 were waited for; matrix products, arithmetic and copies ran while one was open for 11% of the time, Pallas kernels for 0%

profile of v1, /device:TPU:8, one launch (start us, length us, event | category | flops | bytes accessed | tf_op | source)
XLA Modules:
  0.0 1120.7 jit_solution(14985662680587684647)
XLA Ops:
  14.5 6.7 collective-permute-done.6
  23.4 9.5 collective-permute-done.8
  35.6 9.1 collective-permute-done.10
  45.3 11.1 collective-permute-done.12
  56.7 63.0 %all-gather.3.cloned.1.call-done = bf16[1,3200,768]{2,0,1:T(2,128)(2,1)} async-done(((bf16[1,100,768]{2,0,1:T(2,128)(2,1)}), bf16[1,3200,768]{2,0,1:T(2,128)(2,1)}) %all-gather.3.cloned.1.call-update) | async-done | bytes 4915216 | tf_op jit(solution)/shard_map/all_gather | solution.py:101
  126.8 181.3 %while.43 = (s32[]{:T(128)}, bf16[128,768]{1,0:T(8,128)(2,1)}, bf16[2,2,3,64,768]{4,3,2,1,0:T(8,128)(2,1)S(1)}, f32[2,128,768]{2,1,0:T(8,128)}, s32[]{:T(128)}, ...) while((s32[]{:T(128)}, bf16[128,768]{1,0:T(8,128)(2,1)}, ...), condition=%wide.region_3.4_spmd, body=%wide.region_0.3_spmd.sunk | while | flops 1360330752 | bytes 25166232 | solution.py:142
  163.6 10.1 collective-permute-done
  182.9 7.6 conditional.5
  183.4 6.3 multiply_convert_fusion
  207.3 7.5 conditional.5
  207.8 6.3 multiply_convert_fusion
  259.9 6.2 collective-permute-start.2
  270.1 6.8 collective-permute-start
  279.5 6.2 collective-permute-start.2
  311.6 508.9 %while.44 = (s32[]{:T(128)}, bf16[128,768]{1,0:T(8,128)(2,1)S(1)}, bf16[2,128,768]{2,1,0:T(8,128)(2,1)}, bf16[2,128,768]{2,1,0:T(8,128)(2,1)}, s32[]{:T(128)}, /...) while((s32[]{:T(128)}, bf16[128,768]{1,0:T(8,128)(2,1)S(1)}, ...), condition=%wide.region_8.9_spmd.clone, body=%wide.region_4.8_spmd.clone.sunk | while | flops 1424437120 | bytes 46599908 | solution.py:207
  324.9 6.2 collective-permute-start.5
  382.6 6.2 collective-permute-start.5
  400.9 6.6 collective-permute-done.3
  412.6 6.2 collective-permute-start.5
  459.1 160.8 %collective-permute-done.3 = bf16[128,768]{1,0:T(8,128)(2,1)S(1)} collective-permute-done((bf16[128,768]{1,0:T(8,128)(2,1)S(1)}, bf16[128,768]{1,0:T(8,128)(2,1)S(1)}, u32[]{:S(2)}, u32[]{:S(2)}) %collective-permute-start.3) | collective-permute-done | bytes 196640 | tf_op jit(solution)/shard_map/while/body/eval_jaxpr/ppermute | solution.py:27
  619.8 34.1 %conditional.6 = (f32[2,1,64,768]{3,1,2,0:T(1,128)}, bf16[2,2,64,768]{3,1,2,0:T(2,128)(2,1)}, bf16[2,128,768]{2,1,0:T(8,128)(2,1)}) conditional(s32[]{:T(128)} %convert_element_type.205, bf16[2,128,768]{2,1,0:T(8,128)(2,1)} %get-tuple-element.928, (pred[]{:T(512)}, s32[]{:T(128)}, f32[2,128,768]{2,1,0:T(8,128)}, bf16[768,150]{1,0:T(8,128)(2,1)}, ...), branch_computations={%region_5.5_spmd, %region_6.7_spmd} | conditional | flops 1422863744 | bytes 37946536 | solution.py:191
  624.2 7.5 fusion.47
  635.0 12.7 %slice_bitcast_fusion.8 = (f32[2,1,64,768]{3,1,2,0:T(1,128)S(1)}, f32[2,1,64,768]{3,1,2,0:T(1,128)S(1)}, f32[2,1,64,768]{3,1,2,0:T(1,128)S(1)}, f32[2,1,64,768]{...) fusion(f32[2,1,64,9,768]{4,3,2,0,1:T(8,128)} %reshape.209), kind=kLoop, calls=%fused_computation.38 | loop fusion | bytes 7077888 | tf_op jit(solution)/shard_map/while/body/eval_jaxpr/cond/branch_1_fun/squeeze | solution.py:55
  657.1 6.2 collective-permute-start.5
  680.5 34.1 %conditional.6 = (f32[2,1,64,768]{3,1,2,0:T(1,128)}, bf16[2,2,64,768]{3,1,2,0:T(2,128)(2,1)}, bf16[2,128,768]{2,1,0:T(8,128)(2,1)}) conditional(s32[]{:T(128)} %convert_element_type.205, bf16[2,128,768]{2,1,0:T(8,128)(2,1)} %get-tuple-element.928, (pred[]{:T(512)}, s32[]{:T(128)}, f32[2,128,768]{2,1,0:T(8,128)}, bf16[768,150]{1,0:T(8,128)(2,1)}, ...), branch_computations={%region_5.5_spmd, %region_6.7_spmd} | conditional | flops 1422863744 | bytes 37946536 | solution.py:191
  684.9 7.5 fusion.47
  695.6 12.7 %slice_bitcast_fusion.8 = (f32[2,1,64,768]{3,1,2,0:T(1,128)S(1)}, f32[2,1,64,768]{3,1,2,0:T(1,128)S(1)}, f32[2,1,64,768]{3,1,2,0:T(1,128)S(1)}, f32[2,1,64,768]{...) fusion(f32[2,1,64,9,768]{4,3,2,0,1:T(8,128)} %reshape.209), kind=kLoop, calls=%fused_computation.38 | loop fusion | bytes 7077888 | tf_op jit(solution)/shard_map/while/body/eval_jaxpr/cond/branch_1_fun/squeeze | solution.py:55
  743.9 6.3 collective-permute-start.5
  761.8 34.5 %collective-permute-start.3 = (bf16[128,768]{1,0:T(8,128)(2,1)S(1)}, bf16[128,768]{1,0:T(8,128)(2,1)S(1)}, u32[]{:S(2)}, u32[]{:S(2)}) collective-permute-start(bf16[128,768]{1,0:T(8,128)(2,1)S(1)} %get-tuple-element.927), channel_id=1, source_target_pairs={{1,0},{2,1},{3,2},{4,3},{5,4},{6,5},{7,6},{9,8},{10,9},{11,10},{12... | collective-permute-start | bytes 589832 | tf_op jit(solution)/shard_map/while/body/eval_jaxpr/ppermute | solution.py:27
  820.5 9.1 convolution_convert_fusion
  834.8 113.7 %fusion.4 = bf16[104,768]{1,0:T(8,128)(2,1)S(1)} fusion(bf16[3200,768]{1,0:T(8,128)(2,1)} %convolution_convert_fusion.1), kind=kCustom, calls=%all-reduce-scatter | all-reduce-scatter fusion | flops 2555905 | bytes 5075968
  956.9 155.1 %reduce-scatter.4.cloned.1.call-done = bf16[216,768]{1,0:T(8,128)(2,1)} async-done(((bf16[6912,768]{1,0:T(8,128)(2,1)}), bf16[216,768]{1,0:T(8,128)(2,1)}) %reduce-scatter.4.cloned.1.call-update) | async-done | bytes 331792 | tf_op jit(solution)/shard_map/reduce_scatter | solution.py:223
  (350 shorter events, 429.7 us)
Async XLA Ops:
  7.2 112.6 %all-gather.3.cloned.1.call-start = ((), (), s32[]{:S(2)}) async-start(), calls=%async_computation.2 | async-start | bytes 10137600 | tf_op jit(solution)/shard_map/all_gather | solution.py:101
  9.1 1102.9 %reduce-scatter.4.cloned.1.call-start = ((), (), s32[]{:S(2)}) async-start(), calls=%async_computation.1 | async-start | bytes 10948608 | tf_op jit(solution)/shard_map/reduce_scatter | solution.py:223
  9.2 12.0 %collective-permute-start.6 = (bf16[4,2,16,3200]{3,2,1,0:T(8,128)(2,1)}, bf16[4,2,16,3200]{3,2,1,0:T(8,128)(2,1)S(1)}, u32[]{:S(2)}, u32[]{:S(2)}) collective-permute-start(bf16[4,2,16,3200]{3,2,1,0:T(8,128)(2,1)} %param.18), channel_id=1, source_target_pairs={{0,1},{1,2},{2,3},{3,4},{4,5},{5,6},{6,7},{7,0},{8,9},{9,10},{10,1... | collective-permute-start | bytes 2457608 | tf_op jit(solution)/shard_map/ppermute | solution.py:86
  9.2 12.0 %collective-permute-start.7 = (bf16[4,2,16,3200]{3,2,1,0:T(8,128)(2,1)}, bf16[4,2,16,3200]{3,2,1,0:T(8,128)(2,1)S(1)}, u32[]{:S(2)}, u32[]{:S(2)}) collective-permute-start(bf16[4,2,16,3200]{3,2,1,0:T(8,128)(2,1)} %param.18), channel_id=1, source_target_pairs={{0,7},{1,0},{2,1},{3,2},{4,3},{5,4},{6,5},{7,6},{8,15},{9,8},{10,9... | collective-permute-start | bytes 2457608 | tf_op jit(solution)/shard_map/ppermute | solution.py:91
  21.1 11.8 %collective-permute-start.8 = (bf16[4,2,16,3200]{3,2,1,0:T(8,128)(2,1)S(1)}, bf16[4,2,16,3200]{3,2,1,0:T(8,128)(2,1)S(1)}, u32[]{:S(2)}, u32[]{:S(2)}) collective-permute-start(bf16[4,2,16,3200]{3,2,1,0:T(8,128)(2,1)S(1)} %collective-permute-done.6), channel_id=1, source_target_pairs={{0,1},{1,2},{2,3},{3,4},{4,5},{5,6},{6,7},{7,0},{8,9},{9,10},{10,1... | collective-permute-start | bytes 2457608 | tf_op jit(solution)/shard_map/ppermute | solution.py:86
  21.1 11.9 %collective-permute-start.9 = (bf16[4,2,16,3200]{3,2,1,0:T(8,128)(2,1)S(1)}, bf16[4,2,16,3200]{3,2,1,0:T(8,128)(2,1)S(1)}, u32[]{:S(2)}, u32[]{:S(2)}) collective-permute-start(bf16[4,2,16,3200]{3,2,1,0:T(8,128)(2,1)S(1)} %collective-permute-done.7), channel_id=1, source_target_pairs={{0,7},{1,0},{2,1},{3,2},{4,3},{5,4},{6,5},{7,6},{8,15},{9,8},{10,9... | collective-permute-start | bytes 2457608 | tf_op jit(solution)/shard_map/ppermute | solution.py:91
  32.9 11.8 %collective-permute-start.10 = (bf16[4,2,16,3200]{3,2,1,0:T(8,128)(2,1)S(1)}, bf16[4,2,16,3200]{3,2,1,0:T(8,128)(2,1)S(1)}, u32[]{:S(2)}, u32[]{:S(2)}) collective-permute-start(bf16[4,2,16,3200]{3,2,1,0:T(8,128)(2,1)S(1)} %collective-permute-done.8), channel_id=1, source_target_pairs={{0,1},{1,2},{2,3},{3,4},{4,5},{5,6},{6,7},{7,0},{8,9},{9,10},{10,1... | collective-permute-start | bytes 2457608 | tf_op jit(solution)/shard_map/ppermute | solution.py:86
  33.0 12.2 %collective-permute-start.11 = (bf16[4,2,16,3200]{3,2,1,0:T(8,128)(2,1)S(1)}, bf16[4,2,16,3200]{3,2,1,0:T(8,128)(2,1)S(1)}, u32[]{:S(2)}, u32[]{:S(2)}) collective-permute-start(bf16[4,2,16,3200]{3,2,1,0:T(8,128)(2,1)S(1)} %collective-permute-done.9), channel_id=1, source_target_pairs={{0,7},{1,0},{2,1},{3,2},{4,3},{5,4},{6,5},{7,6},{8,15},{9,8},{10,9... | collective-permute-start | bytes 2457608 | tf_op jit(solution)/shard_map/ppermute | solution.py:91
  44.7 11.8 %collective-permute-start.12 = (bf16[4,2,16,3200]{3,2,1,0:T(8,128)(2,1)S(1)}, bf16[4,2,16,3200]{3,2,1,0:T(8,128)(2,1)S(1)}, u32[]{:S(2)}, u32[]{:S(2)}) collective-permute-start(bf16[4,2,16,3200]{3,2,1,0:T(8,128)(2,1)S(1)} %collective-permute-done.10), channel_id=1, source_target_pairs={{0,1},{1,2},{2,3},{3,4},{4,5},{5,6},{6,7},{7,0},{8,9},{9,10},{10,1... | collective-permute-start | bytes 2457608 | tf_op jit(solution)/shard_map/ppermute | solution.py:86
  161.7 12.0 %collective-permute-start = (bf16[128,768]{1,0:T(8,128)(2,1)}, bf16[128,768]{1,0:T(8,128)(2,1)S(1)}, u32[]{:S(2)}, u32[]{:S(2)}) collective-permute-start(bf16[128,768]{1,0:T(8,128)(2,1)} %get-tuple-element.891), channel_id=1, source_target_pairs={{0,1},{1,2},{2,3},{3,4},{4,5},{5,6},{6,7},{8,9},{9,10},{10,11},{11... | collective-permute-start | bytes 589832 | tf_op jit(solution)/shard_map/while/body/eval_jaxpr/ppermute | solution.py:27
  239.6 9.8 collective-permute-start.1
  240.9 9.7 collective-permute-start.2
  323.6 11.3 %collective-permute-start.4 = (bf16[2,1,64,768]{3,1,2,0:T(2,128)(2,1)S(1)}, bf16[2,1,64,768]{3,1,2,0:T(2,128)(2,1)S(1)}, u32[]{:S(2)}, u32[]{:S(2)}) collective-permute-start(bf16[2,1,64,768]{3,1,2,0:T(2,128)(2,1)S(1)} %get-tuple-element.864), channel_id=1, source_target_pairs={{8,0},{16,8},{24,16},{32,24},{40,32},{48,40},{56,48},{64,56},{72,6... | collective-permute-start | bytes 589832 | tf_op jit(solution)/shard_map/while/body/eval_jaxpr/ppermute | solution.py:19
  324.9 11.5 %collective-permute-start.5 = (bf16[2,1,64,768]{3,1,2,0:T(2,128)(2,1)S(1)}, bf16[2,1,64,768]{3,1,2,0:T(2,128)(2,1)S(1)}, u32[]{:S(2)}, u32[]{:S(2)}) collective-permute-start(bf16[2,1,64,768]{3,1,2,0:T(2,128)(2,1)S(1)} %get-tuple-element.865), channel_id=1, source_target_pairs={{0,8},{8,16},{16,24},{24,32},{32,40},{40,48},{48,56},{56,64},{64,7... | collective-permute-start | bytes 589832 | tf_op jit(solution)/shard_map/while/body/eval_jaxpr/ppermute | solution.py:18
  352.5 11.1 collective-permute-start.4
  353.8 11.3 %collective-permute-start.5 = (bf16[2,1,64,768]{3,1,2,0:T(2,128)(2,1)S(1)}, bf16[2,1,64,768]{3,1,2,0:T(2,128)(2,1)S(1)}, u32[]{:S(2)}, u32[]{:S(2)}) collective-permute-start(bf16[2,1,64,768]{3,1,2,0:T(2,128)(2,1)S(1)} %get-tuple-element.865), channel_id=1, source_target_pairs={{0,8},{8,16},{16,24},{24,32},{32,40},{40,48},{48,56},{56,64},{64,7... | collective-permute-start | bytes 589832 | tf_op jit(solution)/shard_map/while/body/eval_jaxpr/ppermute | solution.py:18
  381.3 11.3 %collective-permute-start.4 = (bf16[2,1,64,768]{3,1,2,0:T(2,128)(2,1)S(1)}, bf16[2,1,64,768]{3,1,2,0:T(2,128)(2,1)S(1)}, u32[]{:S(2)}, u32[]{:S(2)}) collective-permute-start(bf16[2,1,64,768]{3,1,2,0:T(2,128)(2,1)S(1)} %get-tuple-element.864), channel_id=1, source_target_pairs={{8,0},{16,8},{24,16},{32,24},{40,32},{48,40},{56,48},{64,56},{72,6... | collective-permute-start | bytes 589832 | tf_op jit(solution)/shard_map/while/body/eval_jaxpr/ppermute | solution.py:19
  382.6 11.5 %collective-permute-start.5 = (bf16[2,1,64,768]{3,1,2,0:T(2,128)(2,1)S(1)}, bf16[2,1,64,768]{3,1,2,0:T(2,128)(2,1)S(1)}, u32[]{:S(2)}, u32[]{:S(2)}) collective-permute-start(bf16[2,1,64,768]{3,1,2,0:T(2,128)(2,1)S(1)} %get-tuple-element.865), channel_id=1, source_target_pairs={{0,8},{8,16},{16,24},{24,32},{32,40},{40,48},{48,56},{56,64},{64,7... | collective-permute-start | bytes 589832 | tf_op jit(solution)/shard_map/while/body/eval_jaxpr/ppermute | solution.py:18
  411.3 12.0 %collective-permute-start.4 = (bf16[2,1,64,768]{3,1,2,0:T(2,128)(2,1)S(1)}, bf16[2,1,64,768]{3,1,2,0:T(2,128)(2,1)S(1)}, u32[]{:S(2)}, u32[]{:S(2)}) collective-permute-start(bf16[2,1,64,768]{3,1,2,0:T(2,128)(2,1)S(1)} %get-tuple-element.864), channel_id=1, source_target_pairs={{8,0},{16,8},{24,16},{32,24},{40,32},{48,40},{56,48},{64,56},{72,6... | collective-permute-start | bytes 589832 | tf_op jit(solution)/shard_map/while/body/eval_jaxpr/ppermute | solution.py:19
  412.6 12.4 %collective-permute-start.5 = (bf16[2,1,64,768]{3,1,2,0:T(2,128)(2,1)S(1)}, bf16[2,1,64,768]{3,1,2,0:T(2,128)(2,1)S(1)}, u32[]{:S(2)}, u32[]{:S(2)}) collective-permute-start(bf16[2,1,64,768]{3,1,2,0:T(2,128)(2,1)S(1)} %get-tuple-element.865), channel_id=1, source_target_pairs={{0,8},{8,16},{16,24},{24,32},{32,40},{40,48},{48,56},{56,64},{64,7... | collective-permute-start | bytes 589832 | tf_op jit(solution)/shard_map/while/body/eval_jaxpr/ppermute | solution.py:18
  439.8 11.1 collective-permute-start.4
  441.1 11.2 %collective-permute-start.5 = (bf16[2,1,64,768]{3,1,2,0:T(2,128)(2,1)S(1)}, bf16[2,1,64,768]{3,1,2,0:T(2,128)(2,1)S(1)}, u32[]{:S(2)}, u32[]{:S(2)}) collective-permute-start(bf16[2,1,64,768]{3,1,2,0:T(2,128)(2,1)S(1)} %get-tuple-element.865), channel_id=1, source_target_pairs={{0,8},{8,16},{16,24},{24,32},{32,40},{40,48},{48,56},{56,64},{64,7... | collective-permute-start | bytes 589832 | tf_op jit(solution)/shard_map/while/body/eval_jaxpr/ppermute | solution.py:18
  457.0 162.8 %collective-permute-start.3 = (bf16[128,768]{1,0:T(8,128)(2,1)S(1)}, bf16[128,768]{1,0:T(8,128)(2,1)S(1)}, u32[]{:S(2)}, u32[]{:S(2)}) collective-permute-start(bf16[128,768]{1,0:T(8,128)(2,1)S(1)} %get-tuple-element.927), channel_id=1, source_target_pairs={{1,0},{2,1},{3,2},{4,3},{5,4},{6,5},{7,6},{9,8},{10,9},{11,10},{12... | collective-permute-start | bytes 589832 | tf_op jit(solution)/shard_map/while/body/eval_jaxpr/ppermute | solution.py:27
  655.8 11.9 %collective-permute-start.4 = (bf16[2,1,64,768]{3,1,2,0:T(2,128)(2,1)S(1)}, bf16[2,1,64,768]{3,1,2,0:T(2,128)(2,1)S(1)}, u32[]{:S(2)}, u32[]{:S(2)}) collective-permute-start(bf16[2,1,64,768]{3,1,2,0:T(2,128)(2,1)S(1)} %get-tuple-element.864), channel_id=1, source_target_pairs={{8,0},{16,8},{24,16},{32,24},{40,32},{48,40},{56,48},{64,56},{72,6... | collective-permute-start | bytes 589832 | tf_op jit(solution)/shard_map/while/body/eval_jaxpr/ppermute | solution.py:19
  657.1 12.4 %collective-permute-start.5 = (bf16[2,1,64,768]{3,1,2,0:T(2,128)(2,1)S(1)}, bf16[2,1,64,768]{3,1,2,0:T(2,128)(2,1)S(1)}, u32[]{:S(2)}, u32[]{:S(2)}) collective-permute-start(bf16[2,1,64,768]{3,1,2,0:T(2,128)(2,1)S(1)} %get-tuple-element.865), channel_id=1, source_target_pairs={{0,8},{8,16},{16,24},{24,32},{32,40},{40,48},{48,56},{56,64},{64,7... | collective-permute-start | bytes 589832 | tf_op jit(solution)/shard_map/while/body/eval_jaxpr/ppermute | solution.py:18
  716.5 11.0 collective-permute-start.4
  717.8 11.2 collective-permute-start.5
  742.6 13.3 %collective-permute-start.4 = (bf16[2,1,64,768]{3,1,2,0:T(2,128)(2,1)S(1)}, bf16[2,1,64,768]{3,1,2,0:T(2,128)(2,1)S(1)}, u32[]{:S(2)}, u32[]{:S(2)}) collective-permute-start(bf16[2,1,64,768]{3,1,2,0:T(2,128)(2,1)S(1)} %get-tuple-element.864), channel_id=1, source_target_pairs={{8,0},{16,8},{24,16},{32,24},{40,32},{48,40},{56,48},{64,56},{72,6... | collective-permute-start | bytes 589832 | tf_op jit(solution)/shard_map/while/body/eval_jaxpr/ppermute | solution.py:19
  743.9 13.2 %collective-permute-start.5 = (bf16[2,1,64,768]{3,1,2,0:T(2,128)(2,1)S(1)}, bf16[2,1,64,768]{3,1,2,0:T(2,128)(2,1)S(1)}, u32[]{:S(2)}, u32[]{:S(2)}) collective-permute-start(bf16[2,1,64,768]{3,1,2,0:T(2,128)(2,1)S(1)} %get-tuple-element.865), channel_id=1, source_target_pairs={{0,8},{8,16},{16,24},{24,32},{32,40},{40,48},{48,56},{56,64},{64,7... | collective-permute-start | bytes 589832 | tf_op jit(solution)/shard_map/while/body/eval_jaxpr/ppermute | solution.py:18
  761.8 37.6 %collective-permute-start.3 = (bf16[128,768]{1,0:T(8,128)(2,1)S(1)}, bf16[128,768]{1,0:T(8,128)(2,1)S(1)}, u32[]{:S(2)}, u32[]{:S(2)}) collective-permute-start(bf16[128,768]{1,0:T(8,128)(2,1)S(1)} %get-tuple-element.927), channel_id=1, source_target_pairs={{1,0},{2,1},{3,2},{4,3},{5,4},{6,5},{7,6},{9,8},{10,9},{11,10},{12... | collective-permute-start | bytes 589832 | tf_op jit(solution)/shard_map/while/body/eval_jaxpr/ppermute | solution.py:27
  803.2 12.0 %collective-permute-start.4 = (bf16[2,1,64,768]{3,1,2,0:T(2,128)(2,1)S(1)}, bf16[2,1,64,768]{3,1,2,0:T(2,128)(2,1)S(1)}, u32[]{:S(2)}, u32[]{:S(2)}) collective-permute-start(bf16[2,1,64,768]{3,1,2,0:T(2,128)(2,1)S(1)} %get-tuple-element.864), channel_id=1, source_target_pairs={{8,0},{16,8},{24,16},{32,24},{40,32},{48,40},{56,48},{64,56},{72,6... | collective-permute-start | bytes 589832 | tf_op jit(solution)/shard_map/while/body/eval_jaxpr/ppermute | solution.py:19
  804.5 11.2 collective-permute-start.5
  (58 other events, 629.1 us)
Sparse Core Ops, SparseCore 0:
  11.2 108.5 all-gather.2
  829.7 282.2 reduce-scatter.3
